TPU v7x, 32 devices: a whole 2x2x4 slice. The times are simulated.
32 devices in a mesh: slab: 4 (over x, core), chan: 8 (over z, y).
Axes of the slice: x: 2, y: 2, z: 4, core: 2. Of those that a mesh axis runs over, the one named last changes fastest.
Arguments:
- inputs: bfloat16 [512, 32, 256], P('chan', 'slab'), may hold values from -6 to 6
- weights: bfloat16 [27, 512, 512], P(None, 'chan', 'slab'), may hold values from -0.0546875 to 0.0546875
- cotangent: bfloat16 [512, 32, 256], P('chan', 'slab'), may hold values from -6 to 6
Outputs:
- outputs: bfloat16 [512, 32, 256], P('chan', 'slab')
- gradient: bfloat16 [512, 32, 256], P('chan', 'slab')
All inputs are finite; a program needn't handle non-finite values.
Results may differ from a plain program's by a relative error of at most 0.0014.
Values may be sent and summed in bfloat16 or wider, within the bound.
A program may use at most 64 MiB of HBM per device.

v0:
```python
import functools

import jax
import jax.numpy as jnp
from jax import lax
from jax.experimental import pallas as pl
from jax.experimental.pallas import tpu as pltpu
from jax.sharding import PartitionSpec as P

ROWS = 8
COLS = 32
TAPS = 27
LANES = 128


def when(cond, fn):
    if cond is None:
        fn()
    else:
        pl.when(cond)(fn)


def both(a, b):
    return b if a is None else a if b is None else jnp.logical_and(a, b)


def gather_kernel(S, Z, Y, r, x_ref, w_ref, p_ref, g_ref, wf_ref, wg_ref,
                  lsem, vsend, ysend, vrecv, hsend, hrecv, wsend, wrecv, psend, fsend, precv):
    n = Z * Y
    planes = x_ref.shape[1]
    s, c = lax.axis_index("slab"), lax.axis_index("chan")
    z, y = lax.div(c, Y), lax.rem(c, Y)
    core = lax.rem(s, 2)
    mate = s + 1 - 2 * core
    ypeer = [z * Y + lax.rem(y + j, Y) for j in range(1, Y)]
    up, down = z < Z - 1, z > 0

    barrier = pltpu.get_barrier_semaphore()
    links = [(up, (s, c + Y)), (down, (s, c - Y))]
    links += [(None, (s, peer)) for peer in ypeer]
    links += [(None, (lax.rem(s + j, S), c)) for j in range(1, S)]
    targets = []
    for xx in range(S // 2):
        for j in range(r):
            to = (2 * xx + lax.rem(c, 2), s * r + j)
            targets.append((jnp.logical_or(to[0] != s, to[1] != c), to, j, xx * r + j))
    sources = []
    for k in range(n // 2):
        frm = (lax.div(c, r), 2 * k + core)
        sources.append((jnp.logical_or(frm[0] != s, frm[1] != c), frm))
    links += [(t[0], t[1]) for t in targets] + sources
    for cond, peer in links:
        when(cond, functools.partial(pl.semaphore_signal, barrier, inc=1, device_id=peer,
                                     device_id_type=pl.DeviceIdType.MESH))
    peers = sum(1 if cond is None else cond.astype(jnp.int32) for cond, _ in links)
    pl.semaphore_wait(barrier, peers)

    sent = []

    def send(cond, src, dst, ssem, rsem, to):
        def make():
            return pltpu.make_async_remote_copy(src_ref=src, dst_ref=dst, send_sem=ssem, recv_sem=rsem,
                                                device_id=to, device_id_type=pl.DeviceIdType.MESH)
        when(cond, lambda: make().start())
        sent.append((cond, make))

    def arrive(cond, dst, sem):
        when(cond, lambda: pltpu.make_async_copy(dst, dst, sem).wait())

    def block(v, slot):
        return g_ref.at[v, pl.ds(1, planes), slot]

    def along(cond, v, slot, src, side):
        ok, to = (up, (s, c + Y)) if side == 0 else (down, (s, c - Y))
        send(both(cond, ok), src, block(v, slot), vsend.at[v, side, slot], vrecv.at[v, slot], to)

    def across(cond, v, slot, src):
        for j, peer in enumerate(ypeer):
            send(cond, src, block(v, slot), ysend.at[v, j, slot], vrecv.at[v, slot], (s, peer))

    def halo(cond, v, slot, first, last):
        send(both(cond, s < S - 1), last, g_ref.at[v, 0, slot], hsend.at[v, 0, slot], hrecv.at[v, 0, slot], (s + 1, c))
        send(both(cond, s > 0), first, g_ref.at[v, planes + 1, slot], hsend.at[v, 1, slot], hrecv.at[v, 1, slot],
             (s - 1, c))

    def landed(cond, v, slot):
        arrive(cond, block(v, slot), vrecv.at[v, slot])

    def rim(cond, v, slot):
        halo(cond, v, slot, g_ref.at[v, 1, slot], g_ref.at[v, planes, slot])

    across(None, 1, c, x_ref.at[1])
    along(None, 0, c, x_ref.at[0], 0)
    along(None, 0, c, x_ref.at[0], 1)
    for cond, to, j, k in targets:
        send(cond, p_ref.at[j], wg_ref.at[c], psend.at[k], precv.at[c], to)
    along(None, 1, c, x_ref.at[1], 0)
    along(None, 1, c, x_ref.at[1], 1)
    across(None, 0, c, x_ref.at[0])
    for j in range(1, S):
        send(None, w_ref, wf_ref.at[s], wsend.at[j], wrecv.at[s], (lax.rem(s + j, S), c))
    for v in range(2):
        pltpu.make_async_copy(x_ref.at[v], block(v, c), lsem.at[v]).start()
        halo(None, v, c, x_ref.at[v, 0], x_ref.at[v, planes - 1])
    pltpu.make_async_copy(w_ref, wf_ref.at[s], lsem.at[2]).start()
    home = jnp.logical_and(s == lax.div(c, r), lax.rem(c, 2) == core)
    when(home, lambda: pltpu.make_async_copy(p_ref.at[lax.rem(c, r)], wg_ref.at[c], precv.at[c]).start())

    for side in range(2):
        def clear(side=side):
            for v in range(2):
                row = 0 if side == 0 else planes + 1
                g_ref[v, row] = jnp.zeros(g_ref.shape[2:], g_ref.dtype)
        when(s == (0 if side == 0 else S - 1), clear)

    for peer in ypeer:
        landed(None, 1, peer)
        along(None, 1, peer, block(1, peer), 0)
        along(None, 1, peer, block(1, peer), 1)
        rim(None, 1, peer)
    for k in range(1, Z):
        for side in range(2):
            zz = z - k if side == 0 else z + k
            have = zz >= 0 if side == 0 else zz < Z
            slot = zz * Y + y
            landed(have, 0, slot)
            if k < Z - 1:
                along(have, 0, slot, block(0, slot), side)
            across(have, 0, slot, block(0, slot))
            rim(have, 0, slot)
            for yy in range(Y):
                slot = zz * Y + yy
                landed(have, 1, slot)
                if k < Z - 1:
                    along(have, 1, slot, block(1, slot), side)
                rim(have, 1, slot)
    for k in range(n // 2):
        slot = 2 * k + core
        arrive(None, wg_ref.at[slot], precv.at[slot])
        send(None, wg_ref.at[slot], wg_ref.at[slot], fsend.at[k], precv.at[slot], (mate, c))
    for peer in ypeer:
        landed(None, 0, peer)
        rim(None, 0, peer)
        for k in range(1, Z):
            for side in range(2):
                zz = z - k if side == 0 else z + k
                have = zz >= 0 if side == 0 else zz < Z
                slot = zz * Y + peer - z * Y
                landed(have, 0, slot)
                rim(have, 0, slot)
    for v in range(2):
        pltpu.make_async_copy(x_ref.at[v], block(v, c), lsem.at[v]).wait()
    pltpu.make_async_copy(w_ref, wf_ref.at[s], lsem.at[2]).wait()
    for j in range(1, S):
        slot = lax.rem(s + j, S)
        arrive(None, wf_ref.at[slot], wrecv.at[slot])
    for k in range(n // 2):
        slot = 2 * k + 1 - core
        arrive(None, wg_ref.at[slot], precv.at[slot])
    for v in range(2):
        for slot in range(n):
            arrive(s > 0, g_ref.at[v, 0, slot], hrecv.at[v, 0, slot])
            arrive(s < S - 1, g_ref.at[v, planes + 1, slot], hrecv.at[v, 1, slot])
    for cond, make in sent:
        when(cond, lambda make=make: make().wait_send())


def conv_kernel(g_ref, wf_ref, wg_ref, o_ref, k_ref):
    S, _, lc, width = wf_ref.shape
    n = wg_ref.shape[0]
    planes = o_ref.shape[1]
    cells = o_ref.shape[3]
    pack = LANES // lc
    for t in range(TAPS):
        rows = pl.ds(t * lc, lc)
        k_ref[0, rows, :] = jnp.concatenate([wf_ref[i, t] for i in range(S)], axis=-1)
        at = (t % pack) * lc
        k_ref[1, rows, :] = jnp.concatenate([wg_ref[i, t // pack][:, at:at + lc] for i in range(n)], axis=-1)
    lane = lax.broadcasted_iota(jnp.int32, (lc, cells), 1)
    row, col = lane // COLS, lane % COLS
    nine = 9 * lc

    def step(k, carry):
        v, d = k // planes, k % planes
        total = None
        for a in range(3):
            part = jnp.dot(k_ref[v, pl.ds(a * nine, nine), :], g_ref[v, d + a], preferred_element_type=jnp.float32)
            total = part if total is None else total + part
        result = None
        for b in range(3):
            lines = None
            for c in range(3):
                at = (3 * b + c) * lc
                piece = total[at:at + lc]
                if c != 1:
                    piece = pltpu.roll(piece, (1 - c) % cells, 1)
                    piece = jnp.where(col == (0 if c == 0 else COLS - 1), 0.0, piece)
                lines = piece if lines is None else lines + piece
            if b != 1:
                lines = pltpu.roll(lines, ((1 - b) * COLS) % cells, 1)
                lines = jnp.where(row == (0 if b == 0 else ROWS - 1), 0.0, lines)
            result = lines if result is None else result + lines
        o_ref[v, d] = result.astype(o_ref.dtype)
        return carry

    lax.fori_loop(0, 2 * planes, step, 0)


def body(S, n, inputs, weights, cotangent):
    lc, planes, cells = inputs.shape
    wide = weights.shape[2]
    r = wide // lc
    C = n * lc
    Y = max(d for d in range(1, n + 1) if n % d == 0 and 2 * d * d <= n)
    Z = n // Y
    volumes = jnp.stack((inputs, cotangent)).transpose(0, 2, 1, 3)
    pack = LANES // lc
    nt = -(-TAPS // pack)
    flipped = jnp.pad(weights[::-1], ((0, nt * pack - TAPS), (0, 0), (0, 0)))
    pieces = flipped.reshape(nt, pack, lc, r, lc).transpose(3, 0, 4, 1, 2).reshape(r, nt, lc, pack * lc)
    vmem = pl.BlockSpec(memory_space=pltpu.VMEM)
    anyspace = pl.BlockSpec(memory_space=pl.ANY)
    dma = pltpu.SemaphoreType.DMA
    bf16 = jnp.bfloat16
    gathered, wf, wg = pl.pallas_call(
        functools.partial(gather_kernel, S, Z, Y, r),
        out_shape=(jax.ShapeDtypeStruct((2, planes + 2, n, lc, cells), bf16),
                   jax.ShapeDtypeStruct((S,) + weights.shape, bf16),
                   jax.ShapeDtypeStruct((n,) + pieces.shape[1:], bf16)),
        in_specs=[anyspace] * 3,
        out_specs=(vmem,) * 3,
        scratch_shapes=[dma((3,)), dma((2, 2, n)), dma((2, Y - 1, n)), dma((2, n)), dma((2, 2, n)), dma((2, 2, n)),
                        dma((S,)), dma((S,)), dma((S // 2 * r,)), dma((n // 2,)), dma((n,))],
        compiler_params=pltpu.CompilerParams(collective_id=0, has_side_effects=True, vmem_limit_bytes=40 << 20),
        name="gather",
    )(volumes, weights, pieces)
    out = pl.pallas_call(
        conv_kernel,
        out_shape=jax.ShapeDtypeStruct((2, planes, lc, cells), bf16),
        in_specs=[vmem] * 3,
        out_specs=vmem,
        scratch_shapes=[pltpu.VMEM((2, TAPS * lc, C), bf16)],
        compiler_params=pltpu.CompilerParams(vmem_limit_bytes=48 << 20),
        name="conv",
    )(gathered.reshape(2, planes + 2, C, cells), wf, wg)
    out = out.transpose(0, 2, 1, 3)
    return out[0], out[1]


def solution(mesh):
    S, n = mesh.shape["slab"], mesh.shape["chan"]
    return jax.shard_map(
        functools.partial(body, S, n),
        mesh=mesh,
        in_specs=(P("chan", "slab", None), P(None, "chan", "slab"), P("chan", "slab", None)),
        out_specs=(P("chan", "slab", None), P("chan", "slab", None)),
        check_vma=False,
    )
```

profile of v0, /device:TPU:1, one launch (start us, length us, event | category | flops | bytes accessed | tf_op | source)
XLA Modules:
  0.0 121.5 jit_solution(12250857680872496528)
XLA Ops:
  0.6 1.0 rev.3
  1.7 0.4 reshape.13
  2.1 0.0 copy-start.2
  2.1 0.0 copy-start.3
  2.1 2.9 %copy.7 = bf16[14,2,64,2,64]{2,1,4,0,3:T(2,128)(2,1)S(1)} copy(bf16[14,2,64,2,64]{4,3,2,1,0:T(2,128)(2,1)S(1)} %reshape.13) | data formatting | bytes 917504 | tf_op jit(solution)/shard_map/reshape | solution.py:220
  5.0 0.0 copy-start.1
  5.0 0.4 reshape.14.p_ref
  5.4 0.0 copy-done.2
  5.4 0.0 copy-done.3
  5.5 0.1 copy_bitcast_fusion
  5.6 0.1 maximum_bitcast_fusion.x_ref
  5.6 0.4 copy-done.1
  6.0 95.8 %gather.1 = (bf16[2,10,8,64,256]{4,3,2,1,0:T(8,128)(2,1)S(1)}, bf16[4,27,64,128]{3,2,1,0:T(8,128)(2,1)S(1)}, bf16[8,14,64,128]{3,2,1,0:T(8,128)(2,1)S(1)}) custom-call(bf16[2,8,64,256]{3,2,1,0:T(8,128)(2,1)S(1)} %maximum_bitcast_fusion.x_ref, bf16[27,64,128]{2,1,0:T(8,128)(2,1)S(1)} %copy-done.1, bf16[2,14,64,128]{3,2,1,0:T(8,128)(2,1)S(1)} %reshape.14.p_ref), custom_call_target="tpu_custom_call" | custom-call | tf_op jit(solution)/shard_map/gather/pallas_call | solution.py:225
  101.8 0.0 copy-start
  101.9 2.3 %copy-done = bf16[2,10,8,64,256]{4,3,2,1,0:T(8,128)(2,1)} copy-done((bf16[2,10,8,64,256]{4,3,2,1,0:T(8,128)(2,1)}, bf16[2,10,8,64,256]{4,3,2,1,0:T(8,128)(2,1)S(1)}, u32[]{:S(2)}) %copy-start) | copy-done | bytes 5242904
  104.2 15.5 %conv.1 = bf16[2,8,64,256]{3,2,1,0:T(8,128)(2,1)S(1)} custom-call(bf16[2,10,512,256]{3,2,1,0:T(8,128)(2,1)} %bitcast.13, bf16[4,27,64,128]{3,2,1,0:T(8,128)(2,1)S(1)} %get-tuple-element.6.wf_ref, bf16[8,14,64,128]{3,2,1,0:T(8,128)(2,1)S(1)} %get-tuple-element.7.wg_ref), custom_call_target="tpu_custom_call" | custom-call | tf_op jit(solution)/shard_map/conv/pallas_call | solution.py:237
  119.7 0.9 copy.9
  120.6 0.9 copy.8
  (2 shorter events, 0.1 us)
Async XLA Ops:
  2.1 3.3 %copy-start.2 = (bf16[64,8,256]{2,1,0:T(8,128)(2,1)S(1)}, bf16[64,8,256]{2,1,0:T(8,128)(2,1)}, u32[]{:S(2)}) copy-start(bf16[64,8,256]{2,1,0:T(8,128)(2,1)} %param.5) | copy-start | bytes 786436
  2.1 3.3 %copy-start.3 = (bf16[64,8,256]{2,1,0:T(8,128)(2,1)S(1)}, bf16[64,8,256]{2,1,0:T(8,128)(2,1)}, u32[]{:S(2)}) copy-start(bf16[64,8,256]{2,1,0:T(8,128)(2,1)} %param.3) | copy-start | bytes 786436
  5.0 1.0 copy-start.1
  101.8 2.3 %copy-start = (bf16[2,10,8,64,256]{4,3,2,1,0:T(8,128)(2,1)}, bf16[2,10,8,64,256]{4,3,2,1,0:T(8,128)(2,1)S(1)}, u32[]{:S(2)}) copy-start(bf16[2,10,8,64,256]{4,3,2,1,0:T(8,128)(2,1)S(1)} %get-tuple-element.5) | copy-start | bytes 15728644
where the time goes:
time: 122 us; the launch traced here: 121 us
  Pallas kernels  111 us (91%)
  local copies, waits for them, and re-layouts  9.3 us (8%)
    pallas_call x1, Pallas kernels, body(): pl.pallas_call(functools.partial(gather_kernel, S, Z, Y, r), out_shape=(j...  95.8 us
    pallas_call x1, Pallas kernels, body(): pl.pallas_call(conv_kernel, out_shape=jax.ShapeDtypeStruct((2, planes, lc...  15.5 us
    unnamed x10, local copies, waits for them, and re-layouts  4.42 us
    reshape x3, local copies, waits for them, and re-layouts, body(): flipped.reshape(nt, pack, lc, r, lc).transpose(3, 0, 4, 1, 2)  3.66 us

commit v1 on v0

--- a/solution.py
+++ b/solution.py
@@ -11,6 +11,7 @@
 COLS = 32
 TAPS = 27
 LANES = 128
+H = 2
 
 
 def when(cond, fn):
@@ -28,6 +29,7 @@
                   lsem, vsend, ysend, vrecv, hsend, hrecv, wsend, wrecv, psend, fsend, precv):
     n = Z * Y
     planes = x_ref.shape[1]
+    units, part = 2 * H, planes // H
     s, c = lax.axis_index("slab"), lax.axis_index("chan")
     z, y = lax.div(c, Y), lax.rem(c, Y)
     core = lax.rem(s, 2)
@@ -67,42 +69,48 @@
     def arrive(cond, dst, sem):
         when(cond, lambda: pltpu.make_async_copy(dst, dst, sem).wait())
 
-    def block(v, slot):
-        return g_ref.at[v, pl.ds(1, planes), slot]
-
-    def along(cond, v, slot, src, side):
+    def own(u):
+        return x_ref.at[u // H, pl.ds(u % H * part, part)]
+
+    def block(u, slot):
+        return g_ref.at[u // H, pl.ds(1 + u % H * part, part), slot]
+
+    def along(cond, u, slot, src, side):
         ok, to = (up, (s, c + Y)) if side == 0 else (down, (s, c - Y))
-        send(both(cond, ok), src, block(v, slot), vsend.at[v, side, slot], vrecv.at[v, slot], to)
-
-    def across(cond, v, slot, src):
+        send(both(cond, ok), src, block(u, slot), vsend.at[u, side, slot], vrecv.at[u, slot], to)
+
+    def across(cond, u, slot, src):
         for j, peer in enumerate(ypeer):
-            send(cond, src, block(v, slot), ysend.at[v, j, slot], vrecv.at[v, slot], (s, peer))
-
-    def halo(cond, v, slot, first, last):
-        send(both(cond, s < S - 1), last, g_ref.at[v, 0, slot], hsend.at[v, 0, slot], hrecv.at[v, 0, slot], (s + 1, c))
-        send(both(cond, s > 0), first, g_ref.at[v, planes + 1, slot], hsend.at[v, 1, slot], hrecv.at[v, 1, slot],
-             (s - 1, c))
-
-    def landed(cond, v, slot):
-        arrive(cond, block(v, slot), vrecv.at[v, slot])
-
-    def rim(cond, v, slot):
-        halo(cond, v, slot, g_ref.at[v, 1, slot], g_ref.at[v, planes, slot])
-
-    across(None, 1, c, x_ref.at[1])
-    along(None, 0, c, x_ref.at[0], 0)
-    along(None, 0, c, x_ref.at[0], 1)
-    for cond, to, j, k in targets:
-        send(cond, p_ref.at[j], wg_ref.at[c], psend.at[k], precv.at[c], to)
-    along(None, 1, c, x_ref.at[1], 0)
-    along(None, 1, c, x_ref.at[1], 1)
-    across(None, 0, c, x_ref.at[0])
-    for j in range(1, S):
-        send(None, w_ref, wf_ref.at[s], wsend.at[j], wrecv.at[s], (lax.rem(s + j, S), c))
-    for v in range(2):
-        pltpu.make_async_copy(x_ref.at[v], block(v, c), lsem.at[v]).start()
-        halo(None, v, c, x_ref.at[v, 0], x_ref.at[v, planes - 1])
-    pltpu.make_async_copy(w_ref, wf_ref.at[s], lsem.at[2]).start()
+            send(cond, src, block(u, slot), ysend.at[u, j, slot], vrecv.at[u, slot], (s, peer))
+
+    def landed(cond, u, slot):
+        arrive(cond, block(u, slot), vrecv.at[u, slot])
+
+    def rim(cond, u, slot, first=None, last=None):
+        v = u // H
+        if u % H == H - 1:
+            last = g_ref.at[v, planes, slot] if last is None else last
+            send(both(cond, s < S - 1), last, g_ref.at[v, 0, slot], hsend.at[v, 0, slot], hrecv.at[v, 0, slot],
+                 (s + 1, c))
+        if u % H == 0:
+            first = g_ref.at[v, 1, slot] if first is None else first
+            send(both(cond, s > 0), first, g_ref.at[v, planes + 1, slot], hsend.at[v, 1, slot], hrecv.at[v, 1, slot],
+                 (s - 1, c))
+
+    for u in range(units):
+        for side in range(2):
+            along(None, u, c, own(u), side)
+        across(None, u, c, own(u))
+        if u == H - 1:
+            for cond, to, j, k in targets:
+                send(cond, p_ref.at[j], wg_ref.at[c], psend.at[k], precv.at[c], to)
+    for j in range(1, S // 2):
+        send(None, w_ref, wf_ref.at[s], wsend.at[j], wrecv.at[s], (lax.rem(s + 2 * j, S), c))
+    send(None, w_ref, wf_ref.at[s], wsend.at[0], wrecv.at[s], (mate, c))
+    for u in range(units):
+        pltpu.make_async_copy(own(u), block(u, c), lsem.at[u]).start()
+        rim(None, u, c, x_ref.at[u // H, 0], x_ref.at[u // H, planes - 1])
+    pltpu.make_async_copy(w_ref, wf_ref.at[s], lsem.at[units]).start()
     home = jnp.logical_and(s == lax.div(c, r), lax.rem(c, 2) == core)
     when(home, lambda: pltpu.make_async_copy(p_ref.at[lax.rem(c, r)], wg_ref.at[c], precv.at[c]).start())
 
@@ -113,46 +121,40 @@
                 g_ref[v, row] = jnp.zeros(g_ref.shape[2:], g_ref.dtype)
         when(s == (0 if side == 0 else S - 1), clear)
 
-    for peer in ypeer:
-        landed(None, 1, peer)
-        along(None, 1, peer, block(1, peer), 0)
-        along(None, 1, peer, block(1, peer), 1)
-        rim(None, 1, peer)
     for k in range(1, Z):
-        for side in range(2):
-            zz = z - k if side == 0 else z + k
-            have = zz >= 0 if side == 0 else zz < Z
-            slot = zz * Y + y
-            landed(have, 0, slot)
-            if k < Z - 1:
-                along(have, 0, slot, block(0, slot), side)
-            across(have, 0, slot, block(0, slot))
-            rim(have, 0, slot)
-            for yy in range(Y):
-                slot = zz * Y + yy
-                landed(have, 1, slot)
+        for u in range(units):
+            for side in range(2):
+                zz = z - k if side == 0 else z + k
+                have = zz >= 0 if side == 0 else zz < Z
+                slot = zz * Y + y
+                landed(have, u, slot)
                 if k < Z - 1:
-                    along(have, 1, slot, block(1, slot), side)
-                rim(have, 1, slot)
+                    along(have, u, slot, block(u, slot), side)
+                across(have, u, slot, block(u, slot))
+                rim(have, u, slot)
+        if k == 1:
+            for j in range(1, S // 2):
+                slot = lax.rem(s + 2 * j, S)
+                arrive(None, wf_ref.at[slot], wrecv.at[slot])
+                send(None, wf_ref.at[slot], wf_ref.at[slot], wsend.at[S // 2 + j], wrecv.at[slot], (mate, c))
     for k in range(n // 2):
         slot = 2 * k + core
         arrive(None, wg_ref.at[slot], precv.at[slot])
         send(None, wg_ref.at[slot], wg_ref.at[slot], fsend.at[k], precv.at[slot], (mate, c))
-    for peer in ypeer:
-        landed(None, 0, peer)
-        rim(None, 0, peer)
-        for k in range(1, Z):
-            for side in range(2):
-                zz = z - k if side == 0 else z + k
-                have = zz >= 0 if side == 0 else zz < Z
-                slot = zz * Y + peer - z * Y
-                landed(have, 0, slot)
-                rim(have, 0, slot)
-    for v in range(2):
-        pltpu.make_async_copy(x_ref.at[v], block(v, c), lsem.at[v]).wait()
-    pltpu.make_async_copy(w_ref, wf_ref.at[s], lsem.at[2]).wait()
-    for j in range(1, S):
-        slot = lax.rem(s + j, S)
+    for k in range(Z):
+        for u in range(units):
+            for peer in ypeer:
+                for side in range(2 if k else 1):
+                    zz = z - k if side == 0 else z + k
+                    have = None if k == 0 else zz >= 0 if side == 0 else zz < Z
+                    slot = zz * Y + peer - z * Y
+                    landed(have, u, slot)
+                    rim(have, u, slot)
+    for u in range(units):
+        pltpu.make_async_copy(own(u), block(u, c), lsem.at[u]).wait()
+    pltpu.make_async_copy(w_ref, wf_ref.at[s], lsem.at[units]).wait()
+    for j in range(S // 2):
+        slot = lax.rem(mate + 2 * j, S)
         arrive(None, wf_ref.at[slot], wrecv.at[slot])
     for k in range(n // 2):
         slot = 2 * k + 1 - core
@@ -174,8 +176,9 @@
     for t in range(TAPS):
         rows = pl.ds(t * lc, lc)
         k_ref[0, rows, :] = jnp.concatenate([wf_ref[i, t] for i in range(S)], axis=-1)
-        at = (t % pack) * lc
-        k_ref[1, rows, :] = jnp.concatenate([wg_ref[i, t // pack][:, at:at + lc] for i in range(n)], axis=-1)
+        f = TAPS - 1 - t
+        at = (f % pack) * lc
+        k_ref[1, rows, :] = jnp.concatenate([wg_ref[i, f // pack][:, at:at + lc] for i in range(n)], axis=-1)
     lane = lax.broadcasted_iota(jnp.int32, (lc, cells), 1)
     row, col = lane // COLS, lane % COLS
     nine = 9 * lc
@@ -216,8 +219,8 @@
     volumes = jnp.stack((inputs, cotangent)).transpose(0, 2, 1, 3)
     pack = LANES // lc
     nt = -(-TAPS // pack)
-    flipped = jnp.pad(weights[::-1], ((0, nt * pack - TAPS), (0, 0), (0, 0)))
-    pieces = flipped.reshape(nt, pack, lc, r, lc).transpose(3, 0, 4, 1, 2).reshape(r, nt, lc, pack * lc)
+    padded = jnp.pad(weights, ((0, nt * pack - TAPS), (0, 0), (0, 0)))
+    pieces = padded.reshape(nt, pack, lc, r, lc).transpose(3, 0, 4, 1, 2).reshape(r, nt, lc, pack * lc)
     vmem = pl.BlockSpec(memory_space=pltpu.VMEM)
     anyspace = pl.BlockSpec(memory_space=pl.ANY)
     dma = pltpu.SemaphoreType.DMA
@@ -229,7 +232,7 @@
                    jax.ShapeDtypeStruct((n,) + pieces.shape[1:], bf16)),
         in_specs=[anyspace] * 3,
         out_specs=(vmem,) * 3,
-        scratch_shapes=[dma((3,)), dma((2, 2, n)), dma((2, Y - 1, n)), dma((2, n)), dma((2, 2, n)), dma((2, 2, n)),
+        scratch_shapes=[dma((2 * H + 1,)), dma((2 * H, 2, n)), dma((2 * H, Y - 1, n)), dma((2 * H, n)), dma((2, 2, n)), dma((2, 2, n)),
                         dma((S,)), dma((S,)), dma((S // 2 * r,)), dma((n // 2,)), dma((n,))],
         compiler_params=pltpu.CompilerParams(collective_id=0, has_side_effects=True, vmem_limit_bytes=40 << 20),
         name="gather",

time: 122 us -> 107 us (0.88)
  Pallas kernels: 111 us -> 96.4 us
    pallas_call x1, Pallas kernels: 95.8 us -> 80.9 us  [body(): pl.pallas_call(functools.partial(gather_kernel, S, Z, Y, r), out_shape=(j...]
where the time goes in v1:
time: 107 us; the launch traced here: 106 us
  Pallas kernels  96.4 us (90%)
  local copies, waits for them, and re-layouts  9.27 us (9%)
    pallas_call x1, Pallas kernels, body(): pl.pallas_call(functools.partial(gather_kernel, S, Z, Y, r), out_shape=(j...  80.9 us
    pallas_call x1, Pallas kernels, body(): pl.pallas_call(conv_kernel, out_shape=jax.ShapeDtypeStruct((2, planes, lc...  15.5 us
    unnamed x10, local copies, waits for them, and re-layouts  4.42 us
    reshape x3, local copies, waits for them, and re-layouts, body(): padded.reshape(nt, pack, lc, r, lc).transpose(3, 0, 4, 1, 2)  3.66 us

profile of v1, /device:TPU:1, one launch (start us, length us, event | category | flops | bytes accessed | tf_op | source)
XLA Modules:
  0.0 106.5 jit_solution(4785031009476423116)
XLA Ops:
  0.6 1.0 pad.4
  1.7 0.4 reshape.13
  2.1 0.0 copy-start.2
  2.1 0.0 copy-start.3
  2.1 2.9 %copy.7 = bf16[14,2,64,2,64]{2,1,4,0,3:T(2,128)(2,1)S(1)} copy(bf16[14,2,64,2,64]{4,3,2,1,0:T(2,128)(2,1)S(1)} %reshape.13) | data formatting | bytes 917504 | tf_op jit(solution)/shard_map/reshape | solution.py:223
  5.0 0.0 copy-start.1
  5.0 0.4 reshape.14.p_ref
  5.4 0.0 copy-done.2
  5.4 0.0 copy-done.3
  5.4 0.1 copy_bitcast_fusion
  5.5 0.1 maximum_bitcast_fusion.x_ref
  5.6 0.4 copy-done.1
  6.0 80.9 %gather.1 = (bf16[2,10,8,64,256]{4,3,2,1,0:T(8,128)(2,1)S(1)}, bf16[4,27,64,128]{3,2,1,0:T(8,128)(2,1)S(1)}, bf16[8,14,64,128]{3,2,1,0:T(8,128)(2,1)S(1)}) custom-call(bf16[2,8,64,256]{3,2,1,0:T(8,128)(2,1)S(1)} %maximum_bitcast_fusion.x_ref, bf16[27,64,128]{2,1,0:T(8,128)(2,1)S(1)} %copy-done.1, bf16[2,14,64,128]{3,2,1,0:T(8,128)(2,1)S(1)} %reshape.14.p_ref), custom_call_target="tpu_custom_call" | custom-call | tf_op jit(solution)/shard_map/gather/pallas_call | solution.py:228
  86.9 0.0 copy-start
  86.9 2.3 %copy-done = bf16[2,10,8,64,256]{4,3,2,1,0:T(8,128)(2,1)} copy-done((bf16[2,10,8,64,256]{4,3,2,1,0:T(8,128)(2,1)}, bf16[2,10,8,64,256]{4,3,2,1,0:T(8,128)(2,1)S(1)}, u32[]{:S(2)}) %copy-start) | copy-done | bytes 5242904
  89.2 15.5 %conv.1 = bf16[2,8,64,256]{3,2,1,0:T(8,128)(2,1)S(1)} custom-call(bf16[2,10,512,256]{3,2,1,0:T(8,128)(2,1)} %bitcast.13, bf16[4,27,64,128]{3,2,1,0:T(8,128)(2,1)S(1)} %get-tuple-element.6.wf_ref, bf16[8,14,64,128]{3,2,1,0:T(8,128)(2,1)S(1)} %get-tuple-element.7.wg_ref), custom_call_target="tpu_custom_call" | custom-call | tf_op jit(solution)/shard_map/conv/pallas_call | solution.py:240
  104.8 0.9 copy.9
  105.6 0.9 copy.8
  (1 shorter events, 0.0 us)
Async XLA Ops:
  2.1 3.3 %copy-start.2 = (bf16[64,8,256]{2,1,0:T(8,128)(2,1)S(1)}, bf16[64,8,256]{2,1,0:T(8,128)(2,1)}, u32[]{:S(2)}) copy-start(bf16[64,8,256]{2,1,0:T(8,128)(2,1)} %param.5) | copy-start | bytes 786436
  2.1 3.3 %copy-start.3 = (bf16[64,8,256]{2,1,0:T(8,128)(2,1)S(1)}, bf16[64,8,256]{2,1,0:T(8,128)(2,1)}, u32[]{:S(2)}) copy-start(bf16[64,8,256]{2,1,0:T(8,128)(2,1)} %param.3) | copy-start | bytes 786436
  5.0 1.0 copy-start.1
  86.9 2.3 %copy-start = (bf16[2,10,8,64,256]{4,3,2,1,0:T(8,128)(2,1)}, bf16[2,10,8,64,256]{4,3,2,1,0:T(8,128)(2,1)S(1)}, u32[]{:S(2)}) copy-start(bf16[2,10,8,64,256]{4,3,2,1,0:T(8,128)(2,1)S(1)} %get-tuple-element.5) | copy-start | bytes 15728644

commit v2 on v1

--- a/solution.py
+++ b/solution.py
@@ -26,7 +26,7 @@
 
 
 def gather_kernel(S, Z, Y, r, x_ref, w_ref, p_ref, g_ref, wf_ref, wg_ref,
-                  lsem, vsend, ysend, vrecv, hsend, hrecv, wsend, wrecv, psend, fsend, precv):
+                  lsem, vsend, ysend, vrecv, hsend, hrecv, wsend, wrecv, psend, fsend, xsend, precv):
     n = Z * Y
     planes = x_ref.shape[1]
     units, part = 2 * H, planes // H
@@ -42,14 +42,17 @@
     links += [(None, (s, peer)) for peer in ypeer]
     links += [(None, (lax.rem(s + j, S), c)) for j in range(1, S)]
     targets = []
-    for xx in range(S // 2):
-        for j in range(r):
-            to = (2 * xx + lax.rem(c, 2), s * r + j)
-            targets.append((jnp.logical_or(to[0] != s, to[1] != c), to, j, xx * r + j))
+    pair = S // 2
+    x = lax.div(s, 2)
+    host = 2 * lax.rem(lax.div(c, 2), pair) + lax.rem(c, 2)
+    for j in range(r):
+        to = (host, s * r + j)
+        targets.append((jnp.logical_or(to[0] != s, to[1] != c), to, j, j))
     sources = []
     for k in range(n // 2):
         frm = (lax.div(c, r), 2 * k + core)
-        sources.append((jnp.logical_or(frm[0] != s, frm[1] != c), frm))
+        other = jnp.logical_or(frm[0] != s, frm[1] != c)
+        sources.append((jnp.logical_and(other, x == k % pair), frm))
     links += [(t[0], t[1]) for t in targets] + sources
     for cond, peer in links:
         when(cond, functools.partial(pl.semaphore_signal, barrier, inc=1, device_id=peer,
@@ -111,7 +114,7 @@
         pltpu.make_async_copy(own(u), block(u, c), lsem.at[u]).start()
         rim(None, u, c, x_ref.at[u // H, 0], x_ref.at[u // H, planes - 1])
     pltpu.make_async_copy(w_ref, wf_ref.at[s], lsem.at[units]).start()
-    home = jnp.logical_and(s == lax.div(c, r), lax.rem(c, 2) == core)
+    home = jnp.logical_and(s == lax.div(c, r), s == host)
     when(home, lambda: pltpu.make_async_copy(p_ref.at[lax.rem(c, r)], wg_ref.at[c], precv.at[c]).start())
 
     for side in range(2):
@@ -137,10 +140,16 @@
                 slot = lax.rem(s + 2 * j, S)
                 arrive(None, wf_ref.at[slot], wrecv.at[slot])
                 send(None, wf_ref.at[slot], wf_ref.at[slot], wsend.at[S // 2 + j], wrecv.at[slot], (mate, c))
-    for k in range(n // 2):
-        slot = 2 * k + core
-        arrive(None, wg_ref.at[slot], precv.at[slot])
-        send(None, wg_ref.at[slot], wg_ref.at[slot], fsend.at[k], precv.at[slot], (mate, c))
+    for direct in range(2):
+        for k in range(n // 2):
+            slot = 2 * k + core
+            have = x == k % pair if direct == 0 else x != k % pair
+            piece = wg_ref.at[slot]
+            arrive(have, piece, precv.at[slot])
+            if direct == 0:
+                for j in range(1, pair):
+                    send(have, piece, piece, xsend.at[j, k], precv.at[slot], (lax.rem(s + 2 * j, S), c))
+            send(have, piece, piece, fsend.at[k], precv.at[slot], (mate, c))
     for k in range(Z):
         for u in range(units):
             for peer in ypeer:
@@ -233,7 +242,7 @@
         in_specs=[anyspace] * 3,
         out_specs=(vmem,) * 3,
         scratch_shapes=[dma((2 * H + 1,)), dma((2 * H, 2, n)), dma((2 * H, Y - 1, n)), dma((2 * H, n)), dma((2, 2, n)), dma((2, 2, n)),
-                        dma((S,)), dma((S,)), dma((S // 2 * r,)), dma((n // 2,)), dma((n,))],
+                        dma((S,)), dma((S,)), dma((r,)), dma((n // 2,)), dma((S // 2, n // 2)), dma((n,))],
         compiler_params=pltpu.CompilerParams(collective_id=0, has_side_effects=True, vmem_limit_bytes=40 << 20),
         name="gather",
     )(volumes, weights, pieces)

time: 107 us -> 100 us (0.935)
  Pallas kernels: 96.4 us -> 89.7 us
    pallas_call x1, Pallas kernels: 80.9 us -> 74.2 us  [body(): pl.pallas_call(functools.partial(gather_kernel, S, Z, Y, r), out_shape=(j...]
where the time goes in v2:
time: 100 us; the launch traced here: 99.8 us
  Pallas kernels  89.7 us (90%)
  local copies, waits for them, and re-layouts  9.27 us (9%)
    pallas_call x1, Pallas kernels, body(): pl.pallas_call(functools.partial(gather_kernel, S, Z, Y, r), out_shape=(j...  74.2 us
    pallas_call x1, Pallas kernels, body(): pl.pallas_call(conv_kernel, out_shape=jax.ShapeDtypeStruct((2, planes, lc...  15.5 us
    unnamed x10, local copies, waits for them, and re-layouts  4.42 us
    reshape x3, local copies, waits for them, and re-layouts, body(): padded.reshape(nt, pack, lc, r, lc).transpose(3, 0, 4, 1, 2)  3.66 us

profile of v2, /device:TPU:1, one launch (start us, length us, event | category | flops | bytes accessed | tf_op | source)
XLA Modules:
  0.0 99.8 jit_solution(986056584762332193)
XLA Ops:
  0.6 1.0 %pad.4 = bf16[28,64,128]{2,1,0:T(8,128)(2,1)S(1)} pad(bf16[27,64,128]{2,1,0:T(8,128)(2,1)} %w_ref.1, bf16[]{:T(256)} %constant.2.clone.1), padding=0_1x0_0x0_0 | pad | bytes 901122 | tf_op jit(solution)/shard_map/jit(_pad)/pad | solution.py:231
  1.7 0.4 reshape.13
  2.1 0.0 copy-start.2
  2.1 0.0 copy-start.3
  2.1 2.9 %copy.7 = bf16[14,2,64,2,64]{2,1,4,0,3:T(2,128)(2,1)S(1)} copy(bf16[14,2,64,2,64]{4,3,2,1,0:T(2,128)(2,1)S(1)} %reshape.13) | data formatting | bytes 917504 | tf_op jit(solution)/shard_map/reshape | solution.py:232
  5.0 0.0 copy-start.1
  5.0 0.4 reshape.14.p_ref
  5.4 0.0 copy-done.2
  5.4 0.0 copy-done.3
  5.4 0.1 copy_bitcast_fusion
  5.5 0.1 maximum_bitcast_fusion.x_ref
  5.6 0.4 copy-done.1
  6.0 74.2 %gather.1 = (bf16[2,10,8,64,256]{4,3,2,1,0:T(8,128)(2,1)S(1)}, bf16[4,27,64,128]{3,2,1,0:T(8,128)(2,1)S(1)}, bf16[8,14,64,128]{3,2,1,0:T(8,128)(2,1)S(1)}) custom-call(bf16[2,8,64,256]{3,2,1,0:T(8,128)(2,1)S(1)} %maximum_bitcast_fusion.x_ref, bf16[27,64,128]{2,1,0:T(8,128)(2,1)S(1)} %copy-done.1, bf16[2,14,64,128]{3,2,1,0:T(8,128)(2,1)S(1)} %reshape.14.p_ref), custom_call_target="tpu_custom_call" | custom-call | tf_op jit(solution)/shard_map/gather/pallas_call | solution.py:237
  80.2 0.0 copy-start
  80.2 2.3 %copy-done = bf16[2,10,8,64,256]{4,3,2,1,0:T(8,128)(2,1)} copy-done((bf16[2,10,8,64,256]{4,3,2,1,0:T(8,128)(2,1)}, bf16[2,10,8,64,256]{4,3,2,1,0:T(8,128)(2,1)S(1)}, u32[]{:S(2)}) %copy-start) | copy-done | bytes 5242904
  82.5 15.5 %conv.1 = bf16[2,8,64,256]{3,2,1,0:T(8,128)(2,1)S(1)} custom-call(bf16[2,10,512,256]{3,2,1,0:T(8,128)(2,1)} %bitcast.13, bf16[4,27,64,128]{3,2,1,0:T(8,128)(2,1)S(1)} %get-tuple-element.6.wf_ref, bf16[8,14,64,128]{3,2,1,0:T(8,128)(2,1)S(1)} %get-tuple-element.7.wg_ref), custom_call_target="tpu_custom_call" | custom-call | tf_op jit(solution)/shard_map/conv/pallas_call | solution.py:249
  98.1 0.9 copy.9
  99.0 0.9 copy.8
  (1 shorter events, 0.0 us)
Async XLA Ops:
  2.1 3.3 %copy-start.2 = (bf16[64,8,256]{2,1,0:T(8,128)(2,1)S(1)}, bf16[64,8,256]{2,1,0:T(8,128)(2,1)}, u32[]{:S(2)}) copy-start(bf16[64,8,256]{2,1,0:T(8,128)(2,1)} %param.5) | copy-start | bytes 786436
  2.1 3.3 %copy-start.3 = (bf16[64,8,256]{2,1,0:T(8,128)(2,1)S(1)}, bf16[64,8,256]{2,1,0:T(8,128)(2,1)}, u32[]{:S(2)}) copy-start(bf16[64,8,256]{2,1,0:T(8,128)(2,1)} %param.3) | copy-start | bytes 786436
  5.0 1.0 %copy-start.1 = (bf16[27,64,128]{2,1,0:T(8,128)(2,1)S(1)}, bf16[27,64,128]{2,1,0:T(8,128)(2,1)}, u32[]{:S(2)}) copy-start(bf16[27,64,128]{2,1,0:T(8,128)(2,1)} %w_ref.1) | copy-start | bytes 1327108
  80.2 2.3 %copy-start = (bf16[2,10,8,64,256]{4,3,2,1,0:T(8,128)(2,1)}, bf16[2,10,8,64,256]{4,3,2,1,0:T(8,128)(2,1)S(1)}, u32[]{:S(2)}) copy-start(bf16[2,10,8,64,256]{4,3,2,1,0:T(8,128)(2,1)S(1)} %get-tuple-element.5) | copy-start | bytes 15728644
